TPU v7x, 256 devices: a whole 4x4x8 slice. The times are simulated.
256 devices in a mesh: tm: 4 (over z_hi), space: 64 (over z_lo, x, y, core).
Axes of the slice: x: 4, y: 4, z: 8 (z_hi: 4, z_lo: 2; z = z_hi * 2 + z_lo), core: 2. Of those that a mesh axis runs over, the one named last changes fastest.
Arguments:
- states: float32 [4, 512, 64, 256], P('tm', 'space'), may hold values from -6 to 6
- conductivity: float32 [512, 64, 256], P('space'), may hold values from 0.4 to 1.6
Outputs:
- updated: float32 [4, 512, 64, 256], P('tm', 'space')
All inputs are finite; a program needn't handle non-finite values.
Results may differ from a plain program's by a relative error of at most 0.0001.
Values sent between devices are 32-bit elements; how exact they have to be, the bound alone decides.
No kernel may reach another device: no remote copies, remote signals or barrier semaphores. Data moves between devices by JAX's collectives and lax.ppermute only.
A program may use at most 64 MiB of HBM per device.

v0:
```python
import jax
import jax.numpy as jnp
from jax import lax
from jax.experimental import pallas as pl
from jax.experimental.pallas import tpu as pltpu
from jax.sharding import PartitionSpec as P


FSTEPS = 4
COARSEN = 4
FINE_RATE = 0.1
COARSE_RATE = FINE_RATE * FSTEPS / 16.0
HALF = 4
F32 = jnp.float32
BF16 = jnp.bfloat16
VMEM_LIMIT = 24 * 1024 * 1024
LANES = 128
ROWS = 64
TOP = 8
PADDED = 80
UNROLL = True
CHUNK = 8


def place():
    k, count = lax.axis_index("space"), lax.axis_size("space")
    inside = lambda i: (i != 0) & (i != count - 1)
    par = k % 2
    return par, inside(k), inside(k + 1 - 2 * par), lax.axis_index("tm")


def own_plane(par, i):
    return i + par * (7 - 2 * i)


def half_plane(par, i):
    return i + par * (3 - 2 * i)


def slow_plane(par, i):
    return (7 - i) + par * (2 * i - 7)


def rows_of(ref, p, h, shift=0):
    return ref[p, h, TOP + shift : TOP + ROWS + shift, :]


def put(ref, p, plane):
    for h in range(2):
        ref[p, h, TOP : TOP + ROWS, :] = plane[:, h * LANES : (h + 1) * LANES]


def blank_margins(ref, planes):
    for p in range(planes):
        for h in range(2):
            ref[p, h, 0:TOP, :] = jnp.zeros((TOP, LANES), F32)
            ref[p, h, TOP + ROWS : PADDED, :] = jnp.zeros((TOP, LANES), F32)


def mirror_margins(ref, p):
    for h in range(2):
        ref[p, h, TOP - 1 : TOP, :] = -ref[p, h, TOP : TOP + 1, :]
        ref[p, h, TOP + ROWS : TOP + ROWS + 1, :] = -ref[p, h, TOP + ROWS - 1 : TOP + ROWS, :]


def lane_turns(a0, a1):
    at = lax.broadcasted_iota(jnp.int32, a0.shape, 1)
    up0, up1 = pltpu.roll(a0, LANES - 1, 1), pltpu.roll(a1, LANES - 1, 1)
    down0, down1 = pltpu.roll(a0, 1, 1), pltpu.roll(a1, 1, 1)
    return (jnp.where(at == LANES - 1, up1, up0), up1), (down0, jnp.where(at == 0, down0, down1)), at


def fill_faces(c, kz, lo, hi, scale, unroll):
    @pl.loop(lo, hi, unroll=unroll)
    def _(p):
        for h in range(2):
            kz[p, h] = (rows_of(c, p, h) + rows_of(c, p + 1, h)) * scale


def fill_coefficients(c, kz, k, lo, hi, scale, unroll):
    @pl.loop(lo, hi, unroll=unroll)
    def _(p):
        a0, a1 = rows_of(c, p, 0), rows_of(c, p, 1)
        (up0, up1), (down0, down1), at = lane_turns(a0, a1)
        up1 = jnp.where(at == LANES - 1, -a1, up1)
        down0 = jnp.where(at == 0, -a0, down0)
        for h, a, up, down in ((0, a0, up0, down0), (1, a1, up1, down1)):
            kxu = (a + rows_of(c, p, h, 1)) * scale
            kxd = (a + rows_of(c, p, h, -1)) * scale
            kyu = (a + up) * scale
            kyd = (a + down) * scale
            k[p, 0, h] = 1.0 - ((kxu + kxd) + (kyu + kyd) + (kz[p, h] + kz[p - 1, h]))
            k[p, 1, h] = kxu
            k[p, 2, h] = kxd
            k[p, 3, h] = kyu
            k[p, 4, h] = kyd


def advance(src, store, kz, k, lo, hi, unroll, shift=0):
    at = lax.broadcasted_iota(jnp.int32, (CHUNK, LANES), 1)

    def some(p):
        q = p - shift
        made = []
        for r in range(0, ROWS, CHUNK):
            cut = lambda ref, i, h, s=0: ref[i, h, TOP + r + s : TOP + r + s + CHUNK, :]
            w = lambda i, h: k[q, i, h, r : r + CHUNK, :]
            v = [cut(src, p, h) for h in range(2)]
            up = [pltpu.roll(v[h], LANES - 1, 1) for h in range(2)]
            down = [pltpu.roll(v[h], 1, 1) for h in range(2)]
            up = [jnp.where(at == LANES - 1, up[1], up[0]), up[1]]
            down = [down[0], jnp.where(at == 0, down[0], down[1])]
            for h in range(2):
                a = w(0, h) * v[h]
                b = kz[q, h, r : r + CHUNK] * cut(src, p + 1, h) + kz[q - 1, h, r : r + CHUNK] * cut(src, p - 1, h)
                d = w(1, h) * cut(src, p, h, 1) + w(2, h) * cut(src, p, h, -1)
                e = w(3, h) * up[h] + w(4, h) * down[h]
                made.append((r, h, (a + b) + (d + e)))
        return made

    @pl.loop(lo, hi, unroll=unroll)
    def _(p):
        for r, h, a in some(p):
            store(p, h, r, a)


def into(ref):
    def store(p, h, r, a):
        ref[p, h, TOP + r : TOP + r + CHUNK, :] = a

    return store


def into_fine(ref, shift):
    def store(p, h, r, a):
        ref[p - shift, h, r : r + CHUNK, :] = a

    return store


def block_sums(ref, first, top):
    parts = []
    for side in range(2):
        for h in range(2):
            total = None
            for p in range(first, first + COARSEN):
                for r in range(COARSEN):
                    term = ref[p, h, pl.ds(top + 32 * side + r, 8, stride=COARSEN), :]
                    total = term if total is None else total + term
            parts.append(total)
    return jnp.concatenate(parts, axis=1)


def mxu(a, b):
    return lax.dot_general(a, b, (((1,), (0,)), ((), ())), preferred_element_type=F32)


def split_dot(a, b):
    high = a.astype(BF16)
    low = (a - high.astype(F32)).astype(BF16)
    return mxu(high, b) + mxu(low, b)


def pooled(sums, pool):
    return split_dot(sums, pool) * (1.0 / COARSEN**3)


def matches(rows, cols, by_row):
    r = lax.broadcasted_iota(jnp.int32, (rows, cols), 0)
    c = lax.broadcasted_iota(jnp.int32, (rows, cols), 1)
    same = r // COARSEN == c if by_row else c // COARSEN == r
    return jnp.where(same, 1.0, 0.0).astype(BF16)


def pack_kernel(v, c, whole, pool, spread, tall, sems):
    copies = [
        pltpu.make_async_copy(src, whole.at[pl.ds(f * 8, 8)], sems.at[f]) for f, src in enumerate((v, c))
    ]
    for copy in copies:
        copy.start()
    pool[...] = matches(*pool.shape, True)
    spread[...] = matches(*spread.shape, False)
    tall[...] = matches(*tall.shape, True)
    for copy in copies:
        copy.wait()


def put_own(par, whole, field, coefficient):
    @pl.loop(0, 8)
    def _(i):
        put(field, i, whole[own_plane(par, i)])
        put(coefficient, i, whole[8 + own_plane(par, i)])


def coarse_kernel(whole, pool, out, v0, c0):
    put_own(place()[0], whole, v0, c0)
    sums = [block_sums(ref, 4 * b, TOP) for ref in (v0, c0) for b in range(2)]
    res = pooled(jnp.concatenate(sums, axis=0), pool[...])
    for i in range(4):
        out[i] = res[8 * i : 8 * i + 8]


def early_kernel(whole, h, pool, a, b, kz, k, fine, end, c0):
    par = place()[0]
    blank_margins(a, 12)
    blank_margins(b, 12)
    put_own(par, whole, a, c0)

    @pl.loop(0, 4)
    def _(i):
        put(a, 8 + i, h[own_plane(par, i)])
        put(c0, 8 + i, h[8 + own_plane(par, i)])

    for i in range(12):
        mirror_margins(c0, i)
    scale = 0.5 * FINE_RATE
    fill_faces(c0, kz, 0, 11, scale, UNROLL)
    fill_coefficients(c0, kz, k, 1, 11, scale, UNROLL)
    advance(a, into(b), kz, k, 1, 11, UNROLL)
    advance(b, into(a), kz, k, 2, 10, UNROLL)
    advance(a, into(b), kz, k, 3, 9, UNROLL)
    advance(b, into_fine(fine, 4), kz, k, 4, 8, UNROLL)
    end[0] = pooled(block_sums(fine, 0, 0), pool[...])


def row_turns(a):
    other = pltpu.roll(a, LANES // 2, 1)
    row = lax.broadcasted_iota(jnp.int32, a.shape, 0)
    up = jnp.where(row == 7, pltpu.roll(other, 7, 0), pltpu.roll(a, 7, 0))
    down = jnp.where(row == 0, pltpu.roll(other, 1, 0), pltpu.roll(a, 1, 0))
    return up, down


def coarse_masks():
    scale = 0.5 * COARSE_RATE
    row = lax.broadcasted_iota(jnp.int32, (8, LANES), 0)
    lane = lax.broadcasted_iota(jnp.int32, (8, LANES), 1)
    left = lane < LANES // 2
    up = jnp.where(left | (row < 7), scale, 0.0)
    down = jnp.where(left & (row == 0), 0.0, scale)
    right = jnp.where(lane % (LANES // 2) == LANES // 2 - 1, 0.0, scale)
    before = jnp.where(lane % (LANES // 2) == 0, 0.0, scale)
    return up, down, right, before


def coarse_weights(c, faces, masks):
    up, down = row_turns(c)
    kxu, kxd = (c + up) * masks[0], (c + down) * masks[1]
    kyu = (c + pltpu.roll(c, LANES - 1, 1)) * masks[2]
    kyd = (c + pltpu.roll(c, 1, 1)) * masks[3]
    return 1.0 - ((kxu + kxd) + (kyu + kyd) + faces), kxu, kxd, kyu, kyd


def coarse_step(v, above, below, face_above, face_below, w):
    up, down = row_turns(v)
    x = w[1] * up + w[2] * down
    y = w[3] * pltpu.roll(v, LANES - 1, 1) + w[4] * pltpu.roll(v, 1, 1)
    return (w[0] * v + (face_above * above + face_below * below)) + (x + y)


def coarse_change(start, cc, faces, i, masks):
    w = coarse_weights(cc[i], faces[i] + faces[i - 1], masks)
    step = coarse_step(start[i], start[i + 1], start[i - 1], faces[i], faces[i - 1], w)
    return jnp.where(place()[3] > 0, step, 0.0)


def jump_kernel(own, theirs, end, mate_end, out):
    start = [own[0], own[1], theirs[1], theirs[0]]
    cc = [own[2], own[3], theirs[3], theirs[2]]
    faces = [(cc[i] + cc[i + 1]) * (0.5 * COARSE_RATE) for i in range(3)]
    masks = coarse_masks()
    out[0] = end[0] - coarse_change(start, cc, faces, 1, masks)
    out[1] = mate_end[0] - coarse_change(start, cc, faces, 2, masks)
    for i in range(3):
        out[2 + i] = cc[i]


def late_kernel(whole, g, a, b, kz, k, pool, own, fine, out, before, v0, c0, w0, kl, kzl, extra):
    par, slow_ok, _, _ = place()
    blank_margins(v0, 14)
    blank_margins(w0, 14)

    @pl.loop(0, 8, unroll=True)
    def _(i):
        put(v0, 7 - i, g[slow_plane(par, i)])
        put(c0, 7 - i, g[8 + slow_plane(par, i)])

    for i in range(2):
        put(v0, 8 + i, whole[own_plane(par, i)])
        put(c0, 8 + i, whole[8 + own_plane(par, i)])
    for i in range(10):
        mirror_margins(c0, i)
    sums = [block_sums(ref, 4 * q, TOP) for ref in (v0, c0) for q in range(2)]
    beyond = pooled(jnp.concatenate(sums, axis=0), pool[...])
    start = [beyond[:8], beyond[8:16], own[0], own[1]]
    cc = [beyond[16:24], beyond[24:], own[2], own[3]]
    faces = [(cc[i] + cc[i + 1]) * (0.5 * COARSE_RATE) for i in range(3)]
    faces[1] = jnp.where(slow_ok, faces[1], 0.0)
    masks = coarse_masks()
    before[0] = start[1]
    stepped = [coarse_change(start, cc, faces, i, masks) for i in (1, 2)]
    scale = 0.5 * FINE_RATE
    fill_faces(c0, kzl, 0, 9, scale, True)
    for h in range(2):
        kzl[7, h] = jnp.where(slow_ok, kzl[7, h], 0.0)
    fill_coefficients(c0, kzl, kl, 1, 9, scale, True)
    advance(v0, into(w0), kzl, kl, 1, 9, True)
    for h in range(2):
        w0[9, h] = b[1, h]
        w0[10, h] = b[2, h]
    advance(w0, into(v0), kzl, kl, 2, 9, True)
    advance(w0, into(v0), kz, k, 9, 10, True, 8)
    for h in range(2):
        v0[10, h] = a[2, h]
        v0[11, h] = a[3, h]
    advance(v0, into(w0), kzl, kl, 3, 9, True)
    advance(v0, into(w0), kz, k, 9, 11, True, 8)
    for h in range(2):
        w0[11, h] = b[3, h]
        w0[12, h] = b[4, h]
    advance(w0, into_fine(extra, 4), kzl, kl, 4, 8, True)
    advance(w0, into_fine(fine, 8), kzl, kl, 8, 9, True)
    advance(w0, into_fine(fine, 8), kz, k, 9, 12, True, 8)
    ends = pooled(jnp.concatenate([block_sums(ref, 0, 0) for ref in (extra, fine)], axis=0), pool[...])
    out[0] = ends[8:] - stepped[1]
    out[1] = ends[:8] - stepped[0]


def weights_kernel(cc, kz, k):
    masks = coarse_masks()
    faces = [(cc[i] + cc[i + 1]) * (0.5 * COARSE_RATE) for i in range(7)]
    faces[2] = jnp.where(place()[1], faces[2], 0.0)
    faces[6] = jnp.where(place()[2], faces[6], 0.0)
    for i in range(7):
        kz[i] = faces[i]
    for i in range(6):
        for f, a in enumerate(coarse_weights(cc[i + 1], faces[i] + faces[i + 1], masks)):
            k[i, f] = a


def final_kernel(far, near, other, own_start, kz, k, spread, tall, lower, upper, out, made, sems):
    par, _, _, slice_at = place()

    def previous(p):
        return jnp.where(par == 1, near[p + 2], other[15 - p])

    def second(p):
        return jnp.where(par == 1, other[6 - p], far[p + 3])

    def first(p):
        return jnp.where(par == 1, far[p + 3], other[6 - p])

    def gate(level, a):
        return jnp.where(slice_at >= level, a, 0.0)

    def grow(d, lo, hi):
        return {
            p: coarse_step(d[p], d[p + 1], d[p - 1], kz[p + 3], kz[p + 2], [k[p + 2, i] for i in range(5)])
            for p in range(lo, hi)
        }

    d = {p: gate(3, first(p)) for p in range(-3, 5)}
    u = grow(d, -2, 4)
    d = {p: u[p] + gate(2, second(p)) for p in range(-2, 4)}
    u = grow(d, -1, 3)
    d = {p: gate(1, u[p] + previous(p) - own_start[p + 1]) for p in range(-1, 3)}
    u = grow(d, 0, 2)
    wide = split_dot(jnp.concatenate([u[0], u[1]], axis=0), spread[...])
    high = wide.astype(BF16)
    low = (wide - high.astype(F32)).astype(BF16)
    change = mxu(tall[...], high) + mxu(tall[...], low)
    copies = []
    for half, fine in ((0, lower), (1, upper)):

        @pl.loop(0, 4, unroll=True)
        def _(i):
            for side in range(2):
                for h in range(2):
                    rows = slice(32 * side, 32 * side + 32)
                    cut = change[32 * half : 32 * half + 32, 256 * side + LANES * h : 256 * side + LANES * (h + 1)]
                    made[half, half_plane(par, i), rows, LANES * h : LANES * (h + 1)] = fine[i, h, rows] + cut

        first = HALF * (par if half == 0 else 1 - par)
        copies.append(pltpu.make_async_copy(made.at[half], out.at[pl.ds(first, HALF)], sems.at[half]))
        copies[-1].start()
    for copy in copies:
        copy.wait()


def call(kernel, outs, scratch, flops, count):
    return pl.pallas_call(
        kernel,
        out_shape=[jax.ShapeDtypeStruct(s, F32) for s in outs],
        in_specs=[pl.BlockSpec(memory_space=pltpu.VMEM)] * count,
        out_specs=[pl.BlockSpec(memory_space=pltpu.VMEM)] * len(outs),
        scratch_shapes=[pltpu.VMEM(s, F32) for s in scratch],
        compiler_params=pltpu.CompilerParams(vmem_limit_bytes=VMEM_LIMIT),
        cost_estimate=pl.CostEstimate(flops=flops, bytes_accessed=flops // 4, transcendentals=0),
    )


def per_device(states, conductivity):
    return iteration(states[0], conductivity)[None]


def iteration(v, c):
    planes, rows, cols = v.shape
    plane = (rows, cols)
    wide, padded, block = (2, ROWS, LANES), (2, PADDED, LANES), (8, LANES)
    count, slices = lax.axis_size("space"), lax.axis_size("tm")

    slow_pairs = [(i, i + 1) for i in range(1, count - 1, 2)]
    slow_pairs += [(b, a) for a, b in slow_pairs]
    fast_pairs = [(i, i ^ 1) for i in range(count)]
    slow = lambda x: lax.ppermute(x, "space", slow_pairs)
    fast = lambda x: lax.ppermute(x, "space", fast_pairs)

    outs = [jax.ShapeDtypeStruct((2 * planes,) + plane, F32)]
    outs += [jax.ShapeDtypeStruct(m, BF16) for m in ((512, LANES), (LANES, 512), (64, 16))]
    whole, pool, spread, tall = pl.pallas_call(
        pack_kernel,
        out_shape=outs,
        in_specs=[pl.BlockSpec(memory_space=pltpu.HBM)] * 2,
        out_specs=[pl.BlockSpec(memory_space=pltpu.VMEM)] * 4,
        scratch_shapes=[pltpu.SemaphoreType.DMA((2,))],
        compiler_params=pltpu.CompilerParams(vmem_limit_bytes=VMEM_LIMIT),
    )(*(pltpu.with_memory_space_constraint(x, pltpu.HBM) for x in (v, c)))
    from_slow = slow(whole)
    from_fast = fast(whole)

    (own,) = call(coarse_kernel, [(4,) + block], [(8,) + padded] * 2, 1_000_000, 2)(whole, pool)
    theirs = fast(own)
    a, b, kz, kk, upper, end = call(
        early_kernel,
        [(12,) + padded, (12,) + padded, (11,) + wide, (11, 5) + wide, (4,) + wide, (1,) + block],
        [(12,) + padded],
        8_000_000,
        3,
    )(whole, from_fast, pool)
    mate_end = fast(end)
    (early,) = call(jump_kernel, [(5,) + block], [], 100_000, 4)(own, theirs, end, mate_end)
    beyond = slow(early)
    lower, jumps, before = call(
        late_kernel,
        [(4,) + wide, (2,) + block, (1,) + block],
        [(14,) + padded] * 3 + [(9, 5) + wide, (9,) + wide, (4,) + wide],
        8_000_000,
        8,
    )(whole, from_slow, a, b, kz, kk, pool, own)
    late = fast(jnp.concatenate([jumps, beyond[:3]]))

    line = jnp.stack(
        [beyond[1], beyond[0], jumps[1], jumps[0], early[0], early[1], late[0], late[1], late[2], late[3]]
    )

    def joined(x, steps):
        pairs = [(a * count + i, b * count + i) for i in range(count) for a, b in steps[i % 2]]
        return lax.ppermute(x, ("tm", "space"), pairs)

    far = joined(line, ([(i, i + 2) for i in range(slices - 2)], [(0, slices - 1)]))
    near = joined(line[1:9], ([], [(i, i + 1) for i in range(slices - 1)]))
    cc = jnp.stack([beyond[4], beyond[3], beyond[2], own[2], own[3], theirs[3], theirs[2], late[4]])
    ckz, ck = call(weights_kernel, [(7,) + block, (6, 5) + block], [], 100_000, 1)(cc)
    own_start = jnp.concatenate([before, own[:2], theirs[1:2]])
    other = fast(jnp.concatenate([far, near]))
    return pl.pallas_call(
        final_kernel,
        out_shape=jax.ShapeDtypeStruct((planes,) + plane, F32),
        in_specs=[pl.BlockSpec(memory_space=pltpu.VMEM)] * 10,
        out_specs=pl.BlockSpec(memory_space=pl.ANY),
        scratch_shapes=[pltpu.VMEM((2, HALF) + plane, F32), pltpu.SemaphoreType.DMA((2,))],
        compiler_params=pltpu.CompilerParams(vmem_limit_bytes=VMEM_LIMIT),
    )(far, near, other, own_start, ckz, ck, spread, tall, lower, upper)


def solution(mesh):
    return jax.shard_map(
        per_device,
        mesh=mesh,
        in_specs=(P("tm", "space", None, None), P("space", None, None)),
        out_specs=P("tm", "space", None, None),
        check_vma=False,
    )
```

profile of v0, /device:TPU:31, one launch (start us, length us, event | category | flops | bytes accessed | tf_op | source)
XLA Modules:
  0.0 40.0 jit_solution(7529097120707780153)
XLA Ops:
  0.0 1.2 %shard_map.28 = (f32[16,64,256]{2,1,0:T(8,128)S(1)}, bf16[512,128]{1,0:T(8,128)(2,1)S(1)}, bf16[128,512]{1,0:T(8,128)(2,1)S(1)}, bf16[64,16]{1,0:T(8,128)(2,1)S(1)}) custom-call(f32[8,64,256]{2,1,0:T(8,128)} %bitcast.2, f32[8,64,256]{2,1,0:T(8,128)} %c.1), custom_call_target="tpu_custom_call" | custom-call | tf_op jit(solution)/shard_map/pallas_call | solution.py:420
  1.2 0.8 %collective-permute-start.1 = (f32[16,64,256]{2,1,0:T(8,128)S(1)}, f32[16,64,256]{2,1,0:T(8,128)S(1)}, u32[]{:S(2)}, u32[]{:S(2)}) collective-permute-start(f32[16,64,256]{2,1,0:T(8,128)S(1)} %get-tuple-element.20.whole), channel_id=1, source_target_pairs={{0,1},{1,0},{2,3},{3,2},{4,5},{5,4},{6,7},{7,6},{8,9},{9,8},{10,11... | collective-permute-start | bytes 3145736 | tf_op jit(solution)/shard_map/ppermute | solution.py:416
  2.0 3.0 %collective-permute-start.4 = (f32[16,64,256]{2,1,0:T(8,128)S(1)}, f32[16,64,256]{2,1,0:T(8,128)S(1)}, u32[]{:S(2)}, u32[]{:S(2)}) collective-permute-start(f32[16,64,256]{2,1,0:T(8,128)S(1)} %get-tuple-element.20.whole), channel_id=1, source_target_pairs={{1,2},{3,4},{5,6},{7,8},{9,10},{11,12},{13,14},{15,16},{17,18},{19... | collective-permute-start | bytes 3145736 | tf_op jit(solution)/shard_map/ppermute | solution.py:415
  5.0 0.3 shard_map.29.own
  5.3 0.1 collective-permute-start
  5.4 0.0 collective-permute-done.1.h
  5.4 2.6 %shard_map.30 = (f32[12,2,80,128]{3,2,1,0:T(8,128)S(1)}, f32[12,2,80,128]{3,2,1,0:T(8,128)S(1)}, f32[11,2,64,128]{3,2,1,0:T(8,128)S(1)}, f32[11,5,2,64,128]{4,3,...) custom-call(f32[16,64,256]{2,1,0:T(8,128)S(1)} %get-tuple-element.20.whole, ...), custom_call_target="tpu_custom_call" | custom-call | flops 8000000 | bytes 2000000 | tf_op jit(solution)/shard_map/pallas_call | solution.py:433
  8.1 0.6 %collective-permute-start.2 = (f32[1,8,128]{2,1,0:T(8,128)S(1)}, f32[1,8,128]{2,1,0:T(8,128)S(1)}, u32[]{:S(2)}, u32[]{:S(2)}) collective-permute-start(f32[1,8,128]{2,1,0:T(8,128)S(1)} %get-tuple-element.22.end), channel_id=1, source_target_pairs={{0,1},{1,0},{2,3},{3,2},{4,5},{5,4},{6,7},{7,6},{8,9},{9,8},{10,11... | collective-permute-start | bytes 12296 | tf_op jit(solution)/shard_map/ppermute | solution.py:416
  8.6 0.0 collective-permute-done.theirs
  8.6 0.8 %collective-permute-done.2.mate_end = f32[1,8,128]{2,1,0:T(8,128)S(1)} collective-permute-done((f32[1,8,128]{2,1,0:T(8,128)S(1)}, f32[1,8,128]{2,1,0:T(8,128)S(1)}, u32[]{:S(2)}, u32[]{:S(2)}) %collective-permute-start.2) | collective-permute-done | bytes 4128 | tf_op jit(solution)/shard_map/ppermute | solution.py:416
  9.4 0.1 shard_map.31
  9.5 6.8 %collective-permute-start.3 = (f32[5,8,128]{2,1,0:T(8,128)S(1)}, f32[5,8,128]{2,1,0:T(8,128)S(1)}, u32[]{:S(2)}, u32[]{:S(2)}) collective-permute-start(f32[5,8,128]{2,1,0:T(8,128)S(1)} %shard_map.31), channel_id=1, source_target_pairs={{1,2},{3,4},{5,6},{7,8},{9,10},{11,12},{13,14},{15,16},{17,18},{19... | collective-permute-start | bytes 61448 | tf_op jit(solution)/shard_map/ppermute | solution.py:415
  16.3 6.0 %collective-permute-done.4.g = f32[16,64,256]{2,1,0:T(8,128)S(1)} collective-permute-done((f32[16,64,256]{2,1,0:T(8,128)S(1)}, f32[16,64,256]{2,1,0:T(8,128)S(1)}, u32[]{:S(2)}, u32[]{:S(2)}) %collective-permute-start.4) | collective-permute-done | bytes 1048608 | tf_op jit(solution)/shard_map/ppermute | solution.py:415
  22.3 2.5 %shard_map.32 = (f32[4,2,64,128]{3,2,1,0:T(8,128)S(1)}, f32[2,8,128]{2,1,0:T(8,128)S(1)}, f32[1,8,128]{2,1,0:T(8,128)S(1)}) custom-call(f32[16,64,256]{2,1,0:T(8,128)S(1)} %get-tuple-element.20.whole, f32[16,64,256]{2,1,0:T(8,128)S(1)} %collective-permute-done.4.g, f32[12,2,80,128]{3,2,1,0:T(8,128)S(1)} %get-tuple-element.23.a, ...), custom_call_target="tpu_custom_call" | custom-call | flops 8000000 | bytes 2000000 | tf_op jit(solution)/shard_map/pallas_call | solution.py:443
  24.8 0.0 collective-permute-done.3
  24.9 0.1 collective-permute-start.5
  25.0 1.1 %collective-permute-done.5 = f32[5,8,128]{2,1,0:T(8,128)S(1)} collective-permute-done((f32[5,8,128]{2,1,0:T(8,128)S(1)}, f32[5,8,128]{2,1,0:T(8,128)S(1)}, u32[]{:S(2)}, u32[]{:S(2)}) %collective-permute-start.5) | collective-permute-done | bytes 20512 | tf_op jit(solution)/shard_map/ppermute | solution.py:416
  26.2 4.9 %collective-permute-start.7 = (f32[8,8,128]{2,1,0:T(8,128)S(1)}, f32[8,8,128]{2,1,0:T(8,128)S(1)}, u32[]{:S(2)}, u32[]{:S(2)}) collective-permute-start(f32[8,8,128]{2,1,0:T(8,128)S(1)} %slice.82), channel_id=1, source_target_pairs={{1,65},{65,129},{129,193},{3,67},{67,131},{131,195},{5,69},{69,133... | collective-permute-start | bytes 98312 | tf_op jit(solution)/shard_map/ppermute | solution.py:458
  31.1 4.3 %collective-permute-start.6 = (f32[10,8,128]{2,1,0:T(8,128)S(1)}, f32[10,8,128]{2,1,0:T(8,128)S(1)}, u32[]{:S(2)}, u32[]{:S(2)}) collective-permute-start(f32[10,8,128]{2,1,0:T(8,128)S(1)} %get-tuple-element.41), channel_id=1, source_target_pairs={{0,128},{64,192},{1,193},{2,130},{66,194},{3,195},{4,132},{68,196}... | collective-permute-start | bytes 122888 | tf_op jit(solution)/shard_map/ppermute | solution.py:458
  35.4 0.0 collective-permute-done.7.near
  35.4 1.1 %collective-permute-done.6.far = f32[10,8,128]{2,1,0:T(8,128)S(1)} collective-permute-done((f32[10,8,128]{2,1,0:T(8,128)S(1)}, f32[10,8,128]{2,1,0:T(8,128)S(1)}, u32[]{:S(2)}, u32[]{:S(2)}) %collective-permute-start.6) | collective-permute-done | bytes 40992 | tf_op jit(solution)/shard_map/ppermute | solution.py:458
  36.5 1.3 %collective-permute-start.8 = (f32[18,8,128]{2,1,0:T(8,128)S(1)}, f32[18,8,128]{2,1,0:T(8,128)S(1)}, u32[]{:S(2)}, u32[]{:S(2)}) collective-permute-start(f32[18,8,128]{2,1,0:T(8,128)S(1)} %pad_maximum_fusion), channel_id=1, source_target_pairs={{0,1},{1,0},{2,3},{3,2},{4,5},{5,4},{6,7},{7,6},{8,9},{9,8},{10,11... | collective-permute-start | bytes 221192 | tf_op jit(solution)/shard_map/ppermute | solution.py:416
  37.8 0.1 shard_map.33
  37.8 0.8 %collective-permute-done.8.other = f32[18,8,128]{2,1,0:T(8,128)S(1)} collective-permute-done((f32[18,8,128]{2,1,0:T(8,128)S(1)}, f32[18,8,128]{2,1,0:T(8,128)S(1)}, u32[]{:S(2)}, u32[]{:S(2)}) %collective-permute-start.8) | collective-permute-done | bytes 73760 | tf_op jit(solution)/shard_map/ppermute | solution.py:416
  38.7 1.4 %shard_map.34 = f32[8,64,256]{2,1,0:T(8,128)} custom-call(f32[10,8,128]{2,1,0:T(8,128)S(1)} %collective-permute-done.6.far, f32[8,8,128]{2,1,0:T(8,128)S(1)} %collective-permute-done.7.near, f32[18,8,128]{2,1,0:T(8,128)S(1)} %collective-permute-done.8.other, f32[4,8,128]{2,1,0:T(8,128)S(1)} %pad_maximum_fusion.2.own_start, ...), custom_call_target="tpu_custom_call" | custom-call | tf_op jit(solution)/shard_map/pallas_call | solution.py:466
  (16 shorter events, 0.1 us)
Async XLA Ops:
  1.2 4.2 %collective-permute-start.1 = (f32[16,64,256]{2,1,0:T(8,128)S(1)}, f32[16,64,256]{2,1,0:T(8,128)S(1)}, u32[]{:S(2)}, u32[]{:S(2)}) collective-permute-start(f32[16,64,256]{2,1,0:T(8,128)S(1)} %get-tuple-element.20.whole), channel_id=1, source_target_pairs={{0,1},{1,0},{2,3},{3,2},{4,5},{5,4},{6,7},{7,6},{8,9},{9,8},{10,11... | collective-permute-start | bytes 3145736 | tf_op jit(solution)/shard_map/ppermute | solution.py:416
  2.0 20.3 %collective-permute-start.4 = (f32[16,64,256]{2,1,0:T(8,128)S(1)}, f32[16,64,256]{2,1,0:T(8,128)S(1)}, u32[]{:S(2)}, u32[]{:S(2)}) collective-permute-start(f32[16,64,256]{2,1,0:T(8,128)S(1)} %get-tuple-element.20.whole), channel_id=1, source_target_pairs={{1,2},{3,4},{5,6},{7,8},{9,10},{11,12},{13,14},{15,16},{17,18},{19... | collective-permute-start | bytes 3145736 | tf_op jit(solution)/shard_map/ppermute | solution.py:415
  5.3 3.3 %collective-permute-start = (f32[4,8,128]{2,1,0:T(8,128)S(1)}, f32[4,8,128]{2,1,0:T(8,128)S(1)}, u32[]{:S(2)}, u32[]{:S(2)}) collective-permute-start(f32[4,8,128]{2,1,0:T(8,128)S(1)} %shard_map.29.own), channel_id=1, source_target_pairs={{0,1},{1,0},{2,3},{3,2},{4,5},{5,4},{6,7},{7,6},{8,9},{9,8},{10,11... | collective-permute-start | bytes 49160 | tf_op jit(solution)/shard_map/ppermute | solution.py:416
  8.1 1.4 %collective-permute-start.2 = (f32[1,8,128]{2,1,0:T(8,128)S(1)}, f32[1,8,128]{2,1,0:T(8,128)S(1)}, u32[]{:S(2)}, u32[]{:S(2)}) collective-permute-start(f32[1,8,128]{2,1,0:T(8,128)S(1)} %get-tuple-element.22.end), channel_id=1, source_target_pairs={{0,1},{1,0},{2,3},{3,2},{4,5},{5,4},{6,7},{7,6},{8,9},{9,8},{10,11... | collective-permute-start | bytes 12296 | tf_op jit(solution)/shard_map/ppermute | solution.py:416
  9.5 15.3 %collective-permute-start.3 = (f32[5,8,128]{2,1,0:T(8,128)S(1)}, f32[5,8,128]{2,1,0:T(8,128)S(1)}, u32[]{:S(2)}, u32[]{:S(2)}) collective-permute-start(f32[5,8,128]{2,1,0:T(8,128)S(1)} %shard_map.31), channel_id=1, source_target_pairs={{1,2},{3,4},{5,6},{7,8},{9,10},{11,12},{13,14},{15,16},{17,18},{19... | collective-permute-start | bytes 61448 | tf_op jit(solution)/shard_map/ppermute | solution.py:415
  24.9 1.3 %collective-permute-start.5 = (f32[5,8,128]{2,1,0:T(8,128)S(1)}, f32[5,8,128]{2,1,0:T(8,128)S(1)}, u32[]{:S(2)}, u32[]{:S(2)}) collective-permute-start(f32[5,8,128]{2,1,0:T(8,128)S(1)} %pad_maximum_fusion.1), channel_id=1, source_target_pairs={{0,1},{1,0},{2,3},{3,2},{4,5},{5,4},{6,7},{7,6},{8,9},{9,8},{10,11... | collective-permute-start | bytes 61448 | tf_op jit(solution)/shard_map/ppermute | solution.py:416
  26.2 9.2 %collective-permute-start.7 = (f32[8,8,128]{2,1,0:T(8,128)S(1)}, f32[8,8,128]{2,1,0:T(8,128)S(1)}, u32[]{:S(2)}, u32[]{:S(2)}) collective-permute-start(f32[8,8,128]{2,1,0:T(8,128)S(1)} %slice.82), channel_id=1, source_target_pairs={{1,65},{65,129},{129,193},{3,67},{67,131},{131,195},{5,69},{69,133... | collective-permute-start | bytes 98312 | tf_op jit(solution)/shard_map/ppermute | solution.py:458
  31.1 5.4 %collective-permute-start.6 = (f32[10,8,128]{2,1,0:T(8,128)S(1)}, f32[10,8,128]{2,1,0:T(8,128)S(1)}, u32[]{:S(2)}, u32[]{:S(2)}) collective-permute-start(f32[10,8,128]{2,1,0:T(8,128)S(1)} %get-tuple-element.41), channel_id=1, source_target_pairs={{0,128},{64,192},{1,193},{2,130},{66,194},{3,195},{4,132},{68,196}... | collective-permute-start | bytes 122888 | tf_op jit(solution)/shard_map/ppermute | solution.py:458
  36.5 2.2 %collective-permute-start.8 = (f32[18,8,128]{2,1,0:T(8,128)S(1)}, f32[18,8,128]{2,1,0:T(8,128)S(1)}, u32[]{:S(2)}, u32[]{:S(2)}) collective-permute-start(f32[18,8,128]{2,1,0:T(8,128)S(1)} %pad_maximum_fusion), channel_id=1, source_target_pairs={{0,1},{1,0},{2,3},{3,2},{4,5},{5,4},{6,7},{7,6},{8,9},{9,8},{10,11... | collective-permute-start | bytes 221192 | tf_op jit(solution)/shard_map/ppermute | solution.py:416
where the time goes:
time: 40.2 us; the launch traced here: 40 us
  starting transfers between devices  21.8 us (54%)
  waiting for transfers between devices  9.84 us (24%)
  Pallas kernels  8.17 us (20%)
    ppermute x2, starting transfers between devices, iteration(): slow = lambda x: lax.ppermute(x, 'space', slow_pairs)  9.77 us
    ppermute x2, starting transfers between devices, joined(): return lax.ppermute(x, ('tm', 'space'), pairs)  9.21 us
    ppermute x2, waiting for transfers between devices, iteration(): slow = lambda x: lax.ppermute(x, 'space', slow_pairs)  6.02 us
    ppermute x5, starting transfers between devices, iteration(): fast = lambda x: lax.ppermute(x, 'space', fast_pairs)  2.77 us
    ppermute x5, waiting for transfers between devices, iteration(): fast = lambda x: lax.ppermute(x, 'space', fast_pairs)  2.76 us
    pallas_call x1, Pallas kernels, iteration(): call(early_kernel, [(12,) + padded, (12,) + padded, (11,) + wide, (11, 5)...  2.64 us
    pallas_call x1, Pallas kernels, iteration(): call(late_kernel, [(4,) + wide, (2,) + block, (1,) + block], [(14,) + pad...  2.48 us
    pallas_call x1, Pallas kernels, iteration(): pl.pallas_call(final_kernel, out_shape=jax.ShapeDtypeStruct((planes,) + p...  1.37 us
  transfers between devices with their start and end apart: 9, of which 5 were waited for; matrix products, arithmetic and copies ran while one was open for 0% of the time, Pallas kernels for 14%

commit v1 on v0

--- a/solution.py
+++ b/solution.py
@@ -371,18 +371,18 @@
     change = mxu(tall[...], high) + mxu(tall[...], low)
     copies = []
     for half, fine in ((0, lower), (1, upper)):
-
-        @pl.loop(0, 4, unroll=True)
-        def _(i):
+        first = HALF * (par if half == 0 else 1 - par)
+        for i in range(HALF):
+            at_plane = half_plane(par, i)
             for side in range(2):
                 for h in range(2):
                     rows = slice(32 * side, 32 * side + 32)
                     cut = change[32 * half : 32 * half + 32, 256 * side + LANES * h : 256 * side + LANES * (h + 1)]
-                    made[half, half_plane(par, i), rows, LANES * h : LANES * (h + 1)] = fine[i, h, rows] + cut
-
-        first = HALF * (par if half == 0 else 1 - par)
-        copies.append(pltpu.make_async_copy(made.at[half], out.at[pl.ds(first, HALF)], sems.at[half]))
-        copies[-1].start()
+                    made[half, i, rows, LANES * h : LANES * (h + 1)] = fine[i, h, rows] + cut
+            copies.append(
+                pltpu.make_async_copy(made.at[half, i], out.at[first + at_plane], sems.at[HALF * half + i])
+            )
+            copies[-1].start()
     for copy in copies:
         copy.wait()
 
@@ -468,7 +468,7 @@
         out_shape=jax.ShapeDtypeStruct((planes,) + plane, F32),
         in_specs=[pl.BlockSpec(memory_space=pltpu.VMEM)] * 10,
         out_specs=pl.BlockSpec(memory_space=pl.ANY),
-        scratch_shapes=[pltpu.VMEM((2, HALF) + plane, F32), pltpu.SemaphoreType.DMA((2,))],
+        scratch_shapes=[pltpu.VMEM((2, HALF) + plane, F32), pltpu.SemaphoreType.DMA((2 * HALF,))],
         compiler_params=pltpu.CompilerParams(vmem_limit_bytes=VMEM_LIMIT),
     )(far, near, other, own_start, ckz, ck, spread, tall, lower, upper)
 

time: 40.2 us -> 40.2 us (level)
  no operation moved by 1% of the time
where the time goes in v1:
time: 40.2 us; the launch traced here: 40 us
  starting transfers between devices  21.8 us (54%)
  waiting for transfers between devices  9.84 us (24%)
  Pallas kernels  8.18 us (20%)
    ppermute x2, starting transfers between devices, iteration(): slow = lambda x: lax.ppermute(x, 'space', slow_pairs)  9.77 us
    ppermute x2, starting transfers between devices, joined(): return lax.ppermute(x, ('tm', 'space'), pairs)  9.21 us
    ppermute x2, waiting for transfers between devices, iteration(): slow = lambda x: lax.ppermute(x, 'space', slow_pairs)  6.02 us
    ppermute x5, starting transfers between devices, iteration(): fast = lambda x: lax.ppermute(x, 'space', fast_pairs)  2.77 us
    ppermute x5, waiting for transfers between devices, iteration(): fast = lambda x: lax.ppermute(x, 'space', fast_pairs)  2.76 us
    pallas_call x1, Pallas kernels, iteration(): call(early_kernel, [(12,) + padded, (12,) + padded, (11,) + wide, (11, 5)...  2.64 us
    pallas_call x1, Pallas kernels, iteration(): call(late_kernel, [(4,) + wide, (2,) + block, (1,) + block], [(14,) + pad...  2.48 us
    pallas_call x1, Pallas kernels, iteration(): pl.pallas_call(final_kernel, out_shape=jax.ShapeDtypeStruct((planes,) + p...  1.38 us
  transfers between devices with their start and end apart: 9, of which 5 were waited for; matrix products, arithmetic and copies ran while one was open for 0% of the time, Pallas kernels for 14%

profile of v1, /device:TPU:31, one launch (start us, length us, event | category | flops | bytes accessed | tf_op | source)
XLA Modules:
  0.0 40.0 jit_solution(10444035336312386005)
XLA Ops:
  0.0 1.2 %shard_map.28 = (f32[16,64,256]{2,1,0:T(8,128)S(1)}, bf16[512,128]{1,0:T(8,128)(2,1)S(1)}, bf16[128,512]{1,0:T(8,128)(2,1)S(1)}, bf16[64,16]{1,0:T(8,128)(2,1)S(1)}) custom-call(f32[8,64,256]{2,1,0:T(8,128)} %bitcast.2, f32[8,64,256]{2,1,0:T(8,128)} %c.1), custom_call_target="tpu_custom_call" | custom-call | tf_op jit(solution)/shard_map/pallas_call | solution.py:420
  1.2 0.8 %collective-permute-start.1 = (f32[16,64,256]{2,1,0:T(8,128)S(1)}, f32[16,64,256]{2,1,0:T(8,128)S(1)}, u32[]{:S(2)}, u32[]{:S(2)}) collective-permute-start(f32[16,64,256]{2,1,0:T(8,128)S(1)} %get-tuple-element.20.whole), channel_id=1, source_target_pairs={{0,1},{1,0},{2,3},{3,2},{4,5},{5,4},{6,7},{7,6},{8,9},{9,8},{10,11... | collective-permute-start | bytes 3145736 | tf_op jit(solution)/shard_map/ppermute | solution.py:416
  2.0 3.0 %collective-permute-start.4 = (f32[16,64,256]{2,1,0:T(8,128)S(1)}, f32[16,64,256]{2,1,0:T(8,128)S(1)}, u32[]{:S(2)}, u32[]{:S(2)}) collective-permute-start(f32[16,64,256]{2,1,0:T(8,128)S(1)} %get-tuple-element.20.whole), channel_id=1, source_target_pairs={{1,2},{3,4},{5,6},{7,8},{9,10},{11,12},{13,14},{15,16},{17,18},{19... | collective-permute-start | bytes 3145736 | tf_op jit(solution)/shard_map/ppermute | solution.py:415
  5.0 0.3 shard_map.29.own
  5.3 0.1 collective-permute-start
  5.4 0.0 collective-permute-done.1.h
  5.4 2.6 %shard_map.30 = (f32[12,2,80,128]{3,2,1,0:T(8,128)S(1)}, f32[12,2,80,128]{3,2,1,0:T(8,128)S(1)}, f32[11,2,64,128]{3,2,1,0:T(8,128)S(1)}, f32[11,5,2,64,128]{4,3,...) custom-call(f32[16,64,256]{2,1,0:T(8,128)S(1)} %get-tuple-element.20.whole, ...), custom_call_target="tpu_custom_call" | custom-call | flops 8000000 | bytes 2000000 | tf_op jit(solution)/shard_map/pallas_call | solution.py:433
  8.1 0.6 %collective-permute-start.2 = (f32[1,8,128]{2,1,0:T(8,128)S(1)}, f32[1,8,128]{2,1,0:T(8,128)S(1)}, u32[]{:S(2)}, u32[]{:S(2)}) collective-permute-start(f32[1,8,128]{2,1,0:T(8,128)S(1)} %get-tuple-element.22.end), channel_id=1, source_target_pairs={{0,1},{1,0},{2,3},{3,2},{4,5},{5,4},{6,7},{7,6},{8,9},{9,8},{10,11... | collective-permute-start | bytes 12296 | tf_op jit(solution)/shard_map/ppermute | solution.py:416
  8.6 0.0 collective-permute-done.theirs
  8.6 0.8 %collective-permute-done.2.mate_end = f32[1,8,128]{2,1,0:T(8,128)S(1)} collective-permute-done((f32[1,8,128]{2,1,0:T(8,128)S(1)}, f32[1,8,128]{2,1,0:T(8,128)S(1)}, u32[]{:S(2)}, u32[]{:S(2)}) %collective-permute-start.2) | collective-permute-done | bytes 4128 | tf_op jit(solution)/shard_map/ppermute | solution.py:416
  9.4 0.1 shard_map.31
  9.5 6.8 %collective-permute-start.3 = (f32[5,8,128]{2,1,0:T(8,128)S(1)}, f32[5,8,128]{2,1,0:T(8,128)S(1)}, u32[]{:S(2)}, u32[]{:S(2)}) collective-permute-start(f32[5,8,128]{2,1,0:T(8,128)S(1)} %shard_map.31), channel_id=1, source_target_pairs={{1,2},{3,4},{5,6},{7,8},{9,10},{11,12},{13,14},{15,16},{17,18},{19... | collective-permute-start | bytes 61448 | tf_op jit(solution)/shard_map/ppermute | solution.py:415
  16.3 6.0 %collective-permute-done.4.g = f32[16,64,256]{2,1,0:T(8,128)S(1)} collective-permute-done((f32[16,64,256]{2,1,0:T(8,128)S(1)}, f32[16,64,256]{2,1,0:T(8,128)S(1)}, u32[]{:S(2)}, u32[]{:S(2)}) %collective-permute-start.4) | collective-permute-done | bytes 1048608 | tf_op jit(solution)/shard_map/ppermute | solution.py:415
  22.3 2.5 %shard_map.32 = (f32[4,2,64,128]{3,2,1,0:T(8,128)S(1)}, f32[2,8,128]{2,1,0:T(8,128)S(1)}, f32[1,8,128]{2,1,0:T(8,128)S(1)}) custom-call(f32[16,64,256]{2,1,0:T(8,128)S(1)} %get-tuple-element.20.whole, f32[16,64,256]{2,1,0:T(8,128)S(1)} %collective-permute-done.4.g, f32[12,2,80,128]{3,2,1,0:T(8,128)S(1)} %get-tuple-element.23.a, ...), custom_call_target="tpu_custom_call" | custom-call | flops 8000000 | bytes 2000000 | tf_op jit(solution)/shard_map/pallas_call | solution.py:443
  24.8 0.0 collective-permute-done.3
  24.9 0.1 collective-permute-start.5
  25.0 1.1 %collective-permute-done.5 = f32[5,8,128]{2,1,0:T(8,128)S(1)} collective-permute-done((f32[5,8,128]{2,1,0:T(8,128)S(1)}, f32[5,8,128]{2,1,0:T(8,128)S(1)}, u32[]{:S(2)}, u32[]{:S(2)}) %collective-permute-start.5) | collective-permute-done | bytes 20512 | tf_op jit(solution)/shard_map/ppermute | solution.py:416
  26.2 4.9 %collective-permute-start.7 = (f32[8,8,128]{2,1,0:T(8,128)S(1)}, f32[8,8,128]{2,1,0:T(8,128)S(1)}, u32[]{:S(2)}, u32[]{:S(2)}) collective-permute-start(f32[8,8,128]{2,1,0:T(8,128)S(1)} %slice.82), channel_id=1, source_target_pairs={{1,65},{65,129},{129,193},{3,67},{67,131},{131,195},{5,69},{69,133... | collective-permute-start | bytes 98312 | tf_op jit(solution)/shard_map/ppermute | solution.py:458
  31.1 4.3 %collective-permute-start.6 = (f32[10,8,128]{2,1,0:T(8,128)S(1)}, f32[10,8,128]{2,1,0:T(8,128)S(1)}, u32[]{:S(2)}, u32[]{:S(2)}) collective-permute-start(f32[10,8,128]{2,1,0:T(8,128)S(1)} %get-tuple-element.41), channel_id=1, source_target_pairs={{0,128},{64,192},{1,193},{2,130},{66,194},{3,195},{4,132},{68,196}... | collective-permute-start | bytes 122888 | tf_op jit(solution)/shard_map/ppermute | solution.py:458
  35.4 0.0 collective-permute-done.7.near
  35.4 1.1 %collective-permute-done.6.far = f32[10,8,128]{2,1,0:T(8,128)S(1)} collective-permute-done((f32[10,8,128]{2,1,0:T(8,128)S(1)}, f32[10,8,128]{2,1,0:T(8,128)S(1)}, u32[]{:S(2)}, u32[]{:S(2)}) %collective-permute-start.6) | collective-permute-done | bytes 40992 | tf_op jit(solution)/shard_map/ppermute | solution.py:458
  36.5 1.3 %collective-permute-start.8 = (f32[18,8,128]{2,1,0:T(8,128)S(1)}, f32[18,8,128]{2,1,0:T(8,128)S(1)}, u32[]{:S(2)}, u32[]{:S(2)}) collective-permute-start(f32[18,8,128]{2,1,0:T(8,128)S(1)} %pad_maximum_fusion), channel_id=1, source_target_pairs={{0,1},{1,0},{2,3},{3,2},{4,5},{5,4},{6,7},{7,6},{8,9},{9,8},{10,11... | collective-permute-start | bytes 221192 | tf_op jit(solution)/shard_map/ppermute | solution.py:416
  37.8 0.1 shard_map.33
  37.8 0.8 %collective-permute-done.8.other = f32[18,8,128]{2,1,0:T(8,128)S(1)} collective-permute-done((f32[18,8,128]{2,1,0:T(8,128)S(1)}, f32[18,8,128]{2,1,0:T(8,128)S(1)}, u32[]{:S(2)}, u32[]{:S(2)}) %collective-permute-start.8) | collective-permute-done | bytes 73760 | tf_op jit(solution)/shard_map/ppermute | solution.py:416
  38.7 1.4 %shard_map.34 = f32[8,64,256]{2,1,0:T(8,128)} custom-call(f32[10,8,128]{2,1,0:T(8,128)S(1)} %collective-permute-done.6.far, f32[8,8,128]{2,1,0:T(8,128)S(1)} %collective-permute-done.7.near, f32[18,8,128]{2,1,0:T(8,128)S(1)} %collective-permute-done.8.other, f32[4,8,128]{2,1,0:T(8,128)S(1)} %pad_maximum_fusion.2.own_start, ...), custom_call_target="tpu_custom_call" | custom-call | tf_op jit(solution)/shard_map/pallas_call | solution.py:466
  (16 shorter events, 0.1 us)
Async XLA Ops:
  1.2 4.2 %collective-permute-start.1 = (f32[16,64,256]{2,1,0:T(8,128)S(1)}, f32[16,64,256]{2,1,0:T(8,128)S(1)}, u32[]{:S(2)}, u32[]{:S(2)}) collective-permute-start(f32[16,64,256]{2,1,0:T(8,128)S(1)} %get-tuple-element.20.whole), channel_id=1, source_target_pairs={{0,1},{1,0},{2,3},{3,2},{4,5},{5,4},{6,7},{7,6},{8,9},{9,8},{10,11... | collective-permute-start | bytes 3145736 | tf_op jit(solution)/shard_map/ppermute | solution.py:416
  2.0 20.3 %collective-permute-start.4 = (f32[16,64,256]{2,1,0:T(8,128)S(1)}, f32[16,64,256]{2,1,0:T(8,128)S(1)}, u32[]{:S(2)}, u32[]{:S(2)}) collective-permute-start(f32[16,64,256]{2,1,0:T(8,128)S(1)} %get-tuple-element.20.whole), channel_id=1, source_target_pairs={{1,2},{3,4},{5,6},{7,8},{9,10},{11,12},{13,14},{15,16},{17,18},{19... | collective-permute-start | bytes 3145736 | tf_op jit(solution)/shard_map/ppermute | solution.py:415
  5.3 3.3 %collective-permute-start = (f32[4,8,128]{2,1,0:T(8,128)S(1)}, f32[4,8,128]{2,1,0:T(8,128)S(1)}, u32[]{:S(2)}, u32[]{:S(2)}) collective-permute-start(f32[4,8,128]{2,1,0:T(8,128)S(1)} %shard_map.29.own), channel_id=1, source_target_pairs={{0,1},{1,0},{2,3},{3,2},{4,5},{5,4},{6,7},{7,6},{8,9},{9,8},{10,11... | collective-permute-start | bytes 49160 | tf_op jit(solution)/shard_map/ppermute | solution.py:416
  8.1 1.4 %collective-permute-start.2 = (f32[1,8,128]{2,1,0:T(8,128)S(1)}, f32[1,8,128]{2,1,0:T(8,128)S(1)}, u32[]{:S(2)}, u32[]{:S(2)}) collective-permute-start(f32[1,8,128]{2,1,0:T(8,128)S(1)} %get-tuple-element.22.end), channel_id=1, source_target_pairs={{0,1},{1,0},{2,3},{3,2},{4,5},{5,4},{6,7},{7,6},{8,9},{9,8},{10,11... | collective-permute-start | bytes 12296 | tf_op jit(solution)/shard_map/ppermute | solution.py:416
  9.5 15.3 %collective-permute-start.3 = (f32[5,8,128]{2,1,0:T(8,128)S(1)}, f32[5,8,128]{2,1,0:T(8,128)S(1)}, u32[]{:S(2)}, u32[]{:S(2)}) collective-permute-start(f32[5,8,128]{2,1,0:T(8,128)S(1)} %shard_map.31), channel_id=1, source_target_pairs={{1,2},{3,4},{5,6},{7,8},{9,10},{11,12},{13,14},{15,16},{17,18},{19... | collective-permute-start | bytes 61448 | tf_op jit(solution)/shard_map/ppermute | solution.py:415
  24.9 1.3 %collective-permute-start.5 = (f32[5,8,128]{2,1,0:T(8,128)S(1)}, f32[5,8,128]{2,1,0:T(8,128)S(1)}, u32[]{:S(2)}, u32[]{:S(2)}) collective-permute-start(f32[5,8,128]{2,1,0:T(8,128)S(1)} %pad_maximum_fusion.1), channel_id=1, source_target_pairs={{0,1},{1,0},{2,3},{3,2},{4,5},{5,4},{6,7},{7,6},{8,9},{9,8},{10,11... | collective-permute-start | bytes 61448 | tf_op jit(solution)/shard_map/ppermute | solution.py:416
  26.2 9.2 %collective-permute-start.7 = (f32[8,8,128]{2,1,0:T(8,128)S(1)}, f32[8,8,128]{2,1,0:T(8,128)S(1)}, u32[]{:S(2)}, u32[]{:S(2)}) collective-permute-start(f32[8,8,128]{2,1,0:T(8,128)S(1)} %slice.82), channel_id=1, source_target_pairs={{1,65},{65,129},{129,193},{3,67},{67,131},{131,195},{5,69},{69,133... | collective-permute-start | bytes 98312 | tf_op jit(solution)/shard_map/ppermute | solution.py:458
  31.1 5.4 %collective-permute-start.6 = (f32[10,8,128]{2,1,0:T(8,128)S(1)}, f32[10,8,128]{2,1,0:T(8,128)S(1)}, u32[]{:S(2)}, u32[]{:S(2)}) collective-permute-start(f32[10,8,128]{2,1,0:T(8,128)S(1)} %get-tuple-element.41), channel_id=1, source_target_pairs={{0,128},{64,192},{1,193},{2,130},{66,194},{3,195},{4,132},{68,196}... | collective-permute-start | bytes 122888 | tf_op jit(solution)/shard_map/ppermute | solution.py:458
  36.5 2.2 %collective-permute-start.8 = (f32[18,8,128]{2,1,0:T(8,128)S(1)}, f32[18,8,128]{2,1,0:T(8,128)S(1)}, u32[]{:S(2)}, u32[]{:S(2)}) collective-permute-start(f32[18,8,128]{2,1,0:T(8,128)S(1)} %pad_maximum_fusion), channel_id=1, source_target_pairs={{0,1},{1,0},{2,3},{3,2},{4,5},{5,4},{6,7},{7,6},{8,9},{9,8},{10,11... | collective-permute-start | bytes 221192 | tf_op jit(solution)/shard_map/ppermute | solution.py:416
